TPU v7x, 128 devices: a whole 4x4x4 slice. The times are simulated.
128 devices in a mesh: expert: 8 (over y, core), tok: 16 (over z, x).
Axes of the slice: x: 4, y: 4, z: 4, core: 2. Of those that a mesh axis runs over, the one named last changes fastest.
Arguments:
- hidden: bfloat16 [8, 4096, 2048], P('expert', 'tok'), may hold values from -40 to 40, as said below
- token_ids: int32 [8, 4096], P('expert', 'tok'), may hold values from 0 to 128004, as said below
- weights: bfloat16 [8, 2048, 8192], P('expert', None, 'tok'), may hold values from -6 to 6
Outputs:
- merged: float32 [2048, 8192], P(None, 'tok')
Inputs may be any that keep to these rules, and one draw needn't show every extreme that they name: `token_ids`: each expert's tokens come in sequences of 128 slots: slot 0 holds 128000, then between 63 and 126 further token ids below 128000, then the padding id 128004 in the remaining slots (one or more). `hidden`: channel scales differ by up to a factor of ten.
All inputs are finite; a program needn't handle non-finite values.
Results may differ from a plain program's by a relative error of at most 0.0017.
Values may be sent and summed in bfloat16 or wider, within the bound.
A program may use at most 256 MiB of HBM per device.

v0:
```python
import jax
import jax.numpy as jnp
from jax import lax
from jax.sharding import PartitionSpec as P

HIGH = lax.Precision.HIGHEST


def product(left_matrix, right_matrix):
    return jnp.dot(left_matrix, right_matrix, preferred_element_type=jnp.float32, precision=HIGH)


def factor_blocks(system):
    width = system.shape[0]
    block_size = min(512, width)
    pieces = width // block_size
    lower = jnp.zeros((width, width), jnp.float32)
    inverses = []
    for which in range(pieces):
        offset = which * block_size
        finish = offset + block_size
        corner = system[offset:finish, offset:finish]
        if which > 0:
            earlier = lower[offset:finish, :offset]
            corner = corner - product(earlier, earlier.T)
        factor_block = jnp.linalg.cholesky(corner)
        inverse = jax.scipy.linalg.solve_triangular(
            factor_block, jnp.eye(block_size, dtype=jnp.float32), lower=True
        )
        inverses.append(inverse)
        lower = lower.at[offset:finish, offset:finish].set(factor_block)
        if finish < width:
            below = system[finish:, offset:finish]
            if which > 0:
                below = below - product(lower[finish:, :offset], earlier.T)
            lower = lower.at[finish:, offset:finish].set(product(below, inverse.T))
    return (lower, inverses, block_size)


def solve_blocks(lower, inverses, block_size, right):
    pieces = len(inverses)
    forward = []
    for which in range(pieces):
        offset = which * block_size
        finish = offset + block_size
        current = right[offset:finish]
        if which > 0:
            current = current - product(
                lower[offset:finish, :offset], jnp.concatenate(forward, axis=0)
            )
        forward.append(product(inverses[which], current))
    backward = [None] * pieces
    for which in range(pieces - 1, -1, -1):
        offset = which * block_size
        finish = offset + block_size
        current = forward[which]
        if which < pieces - 1:
            later = jnp.concatenate(backward[which + 1 :], axis=0)
            current = current - product(lower[finish:, offset:finish].T, later)
        backward[which] = product(inverses[which].T, current)
    return jnp.concatenate(backward, axis=0)


def local(hidden, token_ids, weights):
    tokens = hidden[0]
    weight = weights[0]
    live = token_ids[0] != 128004
    masked = jnp.where(live[:, None], tokens, 0)
    count = lax.psum(jnp.sum(live.astype(jnp.float32)), "tok")
    width = tokens.shape[1]
    band_rows = 1
    piece = lax.all_gather(masked, "tok", axis=0, tiled=True)
    gram_band = jnp.zeros((band_rows, width), jnp.float32)
    upward = jnp.dot(piece, weight, preferred_element_type=jnp.float32).astype(jnp.bfloat16)
    projected = jnp.einsum("td,tc->dc", piece, upward, preferred_element_type=jnp.float32)
    widened = piece.astype(jnp.float32)
    squares = jnp.sum(widened * widened, axis=0)
    projected, squares, gram_band = (projected, squares, gram_band)
    partial_gram = jnp.einsum("td,te->de", masked, masked, preferred_element_type=jnp.float32)
    total = lax.psum(partial_gram / count, ("expert", "tok"))
    system = jnp.where(jnp.eye(width, dtype=bool), total, 0.9 * total)
    lower, inverses, block_size = factor_blocks(system)
    terms = (0.9 * projected + 0.1 * squares[:, None] * weight.astype(jnp.float32)) / count
    return solve_blocks(lower, inverses, block_size, lax.psum(terms, "expert"))


def solution(mesh):
    return jax.shard_map(
        local,
        mesh=mesh,
        in_specs=(P("expert", "tok", None), P("expert", "tok"), P("expert", None, "tok")),
        out_specs=P(None, "tok"),
        check_vma=False,
    )
```

profile of v0, /device:TPU:1, one launch (start us, length us, event | category | flops | bytes accessed | tf_op | source)
XLA Modules:
  0.0 1180.8 jit_solution(7761944321056890056)
XLA Ops:
  8.7 36.0 %psum.21 = f32[]{:T(128)} all-reduce(f32[]{:T(128)} %convert_reduce_fusion), channel_id=1, replica_groups=mesh['expert'=8,'tok'=16] {'tok'}, use_global_device_ids=true, to_apply=%region_1.2 | all-reduce | flops 1 | bytes 8 | tf_op jit(solution)/shard_map/psum | solution.py:69
  44.6 10.5 broadcast_divide_fusion
  57.6 291.8 %all-reduce.5.cloned.1.call-done = f32[2048,2048]{0,1:T(8,128)} async-done(((f32[2048,2048]{0,1:T(8,128)}), f32[2048,2048]{0,1:T(8,128)}) %all-reduce.5.cloned.1.call-update) | async-done | bytes 16777232 | tf_op jit(solution)/shard_map/psum | solution.py:80
  349.5 7.2 multiply_select_fusion
  356.7 5.7 copy-done
  364.3 11.7 cholesky.462
  376.1 9.8 custom-call.35
  386.7 11.7 cholesky.481
  398.4 10.0 custom-call.36
  409.1 11.7 cholesky.502
  420.8 9.8 custom-call.37
  431.3 11.7 cholesky.519
  449.1 11.6 while.15
  460.7 39.3 %custom-call.38 = f32[4,128,128]{1,2,0:T(8,128)S(1)} custom-call(f32[4,128,128]{2,1,0:T(8,128)S(1)} %get-tuple-element.117), custom_call_target="InvertDiagBlocksLowerTriangular" | custom-call | tf_op jit(solution)/shard_map/jit(_solve_triangular)/triangular_solve | solution.py:27
  500.0 7.9 scatter.20
  513.7 13.1 %constant_dynamic-update-slice_fusion.16 = (f32[2048,2048]{1,0:T(8,128)}, f32[1536,512]{1,0:T(8,128)S(1)}) fusion(f32[2048,2048]{1,0:T(8,128)} %scatter.20, f32[128,512]{1,0:T(8,128)S(1)} %fusion.187, f32[128,512]{1,0:T(8,128)S(1)} %fusion.188, f32[128,512]{1,0:T(8,128)S(1)} %fusion.190, f32[128,512]{1,0:T(8,128)S(1)} %fusion.133, f32[2048,2048]{0,1:T(8,128)} %copy-done), kind=kOutput, calls=%fused_computation.326 | convolution fusion | flops 4832624640 | bytes 10485760 | tf_op jit(solution)/shard_map/dot_general | solution.py:10
  528.5 3.1 convolution_subtract_fusion.2
  535.3 11.7 cholesky.534
  547.2 9.8 custom-call.39
  559.6 12.1 %cholesky.553 = f32[128,128]{1,0:T(8,128)S(1)} custom-call(f32[128,128]{1,0:T(8,128)S(1)} %cholesky.763), custom_call_target="Cholesky" | custom-call | tf_op jit(solution)/shard_map/jit(cholesky)/cholesky | solution.py:26
  571.7 9.8 custom-call.40
  583.1 11.7 cholesky.574
  594.8 9.8 custom-call.41
  606.1 11.9 %cholesky.591 = f32[128,128]{1,0:T(8,128)S(1)} custom-call(f32[128,128]{1,0:T(8,128)S(1)} %convolution_subtract_fusion.25), custom_call_target="Cholesky" | custom-call | tf_op jit(solution)/shard_map/jit(cholesky)/cholesky | solution.py:26
  625.0 11.6 while.16
  636.6 39.3 %custom-call.42 = f32[4,128,128]{1,2,0:T(8,128)S(1)} custom-call(f32[4,128,128]{2,1,0:T(8,128)S(1)} %get-tuple-element.118), custom_call_target="InvertDiagBlocksLowerTriangular" | custom-call | tf_op jit(solution)/shard_map/jit(_solve_triangular)/triangular_solve | solution.py:27
  681.8 5.5 fusion.24
  687.3 10.1 fusion.37
  697.4 11.6 copy.55
  709.0 6.9 fusion.38
  715.9 2.6 copy.9
  721.3 11.7 cholesky.606
  734.1 9.8 custom-call.43
  747.1 11.9 %cholesky.625 = f32[128,128]{1,0:T(8,128)S(1)} custom-call(f32[128,128]{1,0:T(8,128)S(1)} %cholesky.776), custom_call_target="Cholesky" | custom-call | tf_op jit(solution)/shard_map/jit(cholesky)/cholesky | solution.py:26
  759.6 9.8 custom-call.44
  771.8 11.7 cholesky.646
  784.2 9.8 custom-call.45
  796.2 12.1 %cholesky.663 = f32[128,128]{1,0:T(8,128)S(1)} custom-call(f32[128,128]{1,0:T(8,128)S(1)} %convolution_subtract_fusion.24), custom_call_target="Cholesky" | custom-call | tf_op jit(solution)/shard_map/jit(cholesky)/cholesky | solution.py:26
  813.9 2.8 fusion.77
  816.8 11.6 while.17
  828.4 39.3 %custom-call.46 = f32[4,128,128]{1,2,0:T(8,128)S(1)} custom-call(f32[4,128,128]{2,1,0:T(8,128)S(1)} %get-tuple-element.119), custom_call_target="InvertDiagBlocksLowerTriangular" | custom-call | tf_op jit(solution)/shard_map/jit(_solve_triangular)/triangular_solve | solution.py:27
  876.4 6.1 fusion.41
  882.5 4.9 constant_dynamic-update-slice_fusion.17
  887.5 9.2 fusion.66
  896.7 2.6 copy.11
  902.0 11.7 cholesky.678
  914.8 9.8 custom-call.47
  928.5 11.7 cholesky.697
  940.9 10.2 custom-call.48
  954.3 11.7 cholesky.718
  966.7 9.8 custom-call.49
  978.7 11.7 cholesky.735
  998.6 7.4 multiply_reduce_fusion
  1006.1 47.9 %add_divide_fusion = f32[2048,512]{1,0:T(8,128)} fusion(bf16[4096,2048]{1,0:T(8,128)(2,1)} %all-gather.2.cloned.1.call-done, bf16[1,2048,512]{2,1,0:T(8,128)(2,1)} %param.22, f32[]{:T(128)} %psum.21, f32[2048]{0:T(1024)S(1)} %broadcast_multiply_fusion), kind=kOutput, calls=%fused_computation.14 | convolution fusion | flops 17187209216 | bytes 23076868 | tf_op jit(solution)/shard_map/td,tc->dc/dot_general | solution.py:75
  1054.0 12.0 %while.18 = (s32[]{:T(128)}, f32[512,512]{1,0:T(8,128)}, s32[4,2]{0,1:T(2,128)S(1)}, f32[4,128,128]{2,1,0:T(8,128)S(1)}, s32[]{:T(128)}) while((s32[]{:T(128)}, f32[512,512]{1,0:T(8,128)}, s32[4,2]{0,1:T(2,128)S(1)}, f32[4,128,128]{2,1,0:T(8,128)S(1)}, s32[]{:T(128)}) %tuple.146), condition=%wide.while_cond.7.clone.2, body=%wide.while_body.7.clone.2.sunk | while | flops 2 | bytes 131181 | solution.py:27
  1066.0 39.9 %custom-call.50 = f32[4,128,128]{1,2,0:T(8,128)} custom-call(f32[4,128,128]{2,1,0:T(8,128)S(1)} %get-tuple-element.120), custom_call_target="InvertDiagBlocksLowerTriangular" | custom-call | tf_op jit(solution)/shard_map/jit(_solve_triangular)/triangular_solve | solution.py:27
  1116.1 6.9 all-reduce.7.cloned.1.call-done
  1123.0 3.2 fusion.70
  1126.1 3.5 convolution_subtract_fusion.1
  1129.7 2.9 fusion.155
  1132.6 5.1 fusion.51
  1139.8 7.1 fusion.56
  1154.5 5.3 fusion.46
  1161.7 7.1 fusion.61
  (228 shorter events, 155.8 us)
Async XLA Ops:
  7.4 342.1 %all-reduce.5.cloned.1.call-start = ((), (), s32[]{:S(2)}) async-start(), calls=%async_computation | async-start | bytes 33554432 | tf_op jit(solution)/shard_map/psum | solution.py:80
  55.1 1.2 copy-start.20
  55.1 943.5 %all-gather.2.cloned.1.call-start = ((), (), s32[]{:S(2)}) async-start(), calls=%async_computation.1 | async-start | bytes 17825792 | tf_op jit(solution)/shard_map/all_gather | solution.py:72
  57.5 1065.5 %all-reduce.7.cloned.1.call-start = ((), (), s32[]{:S(2)}) async-start(), calls=%async_computation.2 | async-start | bytes 8388608 | tf_op jit(solution)/shard_map/psum | solution.py:84
  356.7 5.7 copy-start
  513.7 13.1 %copy-start.6 = (f32[128,512]{1,0:T(8,128)}, f32[128,512]{1,0:T(8,128)S(1)}, u32[]{:S(2)}) copy-start(f32[128,512]{1,0:T(8,128)S(1)} %fusion.187) | copy-start | bytes 786436
  526.8 1.7 copy-start.1
  534.3 1.0 copy-start.16
  681.8 15.6 %copy-start.8 = (f32[128,512]{1,0:T(8,128)}, f32[128,512]{1,0:T(8,128)S(1)}, u32[]{:S(2)}) copy-start(f32[128,512]{1,0:T(8,128)S(1)} %fusion.181) | copy-start | bytes 786436
  720.2 1.0 copy-start.17
  867.7 0.7 copy-start.22
  873.5 9.1 copy-start.2
  876.4 11.1 copy-start.10
  901.0 1.0 copy-start.18
  927.8 0.7 copy-start.21
  1109.7 4.4 copy-start.4
  1112.4 1.7 copy-start.12
  1126.1 6.4 copy-start.14
  1129.7 8.0 copy-start.3
  1129.7 8.0 copy-start.11
  1139.8 7.2 copy-start.5
  1139.8 7.2 copy-start.13
  1139.8 7.2 copy-start.19
  1146.9 3.7 copy-start.15
  1152.6 7.2 copy-start.9
  1161.7 7.1 copy-start.7
Sparse Core Ops, SparseCore 0:
  55.3 294.1 all-reduce.4
Sparse Core Ops, SparseCore 1:
  57.8 123.3 all-gather.1
  1054.1 68.9 all-reduce.6
where the time goes:
time: 1190 us; the launch traced here: 1180 us
  other arithmetic  513 us (43%)
  waiting for transfers between devices  299 us (25%)
  matrix products  218 us (18%)
  local copies, waits for them, and re-layouts  87.9 us (7%)
  blocking collectives  36 us (3%)
  between operations  26.2 us (2%)
    another operation x59, other arithmetic, factor_blocks(): factor_block = jnp.linalg.cholesky(corner)  321 us
    psum x1, waiting for transfers between devices, local(): total = lax.psum(partial_gram / count, ('expert', 'tok'))  292 us
    another operation x9, other arithmetic, factor_blocks(): jax.scipy.linalg.solve_triangular(factor_block, jnp.eye(block_size, dtype...  166 us
    dot_general x22, matrix products, product(): jnp.dot(left_matrix, right_matrix, preferred_element_type=jnp.float32, pr...  106 us
    dot_general x1, matrix products, local(): jnp.einsum('td,tc->dc', piece, upward, preferred_element_type=jnp.float32)  47.9 us
    another operation x53, local copies, waits for them, and re-layouts, factor_blocks(): jax.scipy.linalg.solve_triangular(factor_block, jnp.eye(block_size, dtype...  46.5 us
    psum x1, blocking collectives, local(): count = lax.psum(jnp.sum(live.astype(jnp.float32)), 'tok')  36 us
    another operation x28, matrix products, factor_blocks(): jax.scipy.linalg.solve_triangular(factor_block, jnp.eye(block_size, dtype...  30 us
  transfers between devices with their start and end apart: 3, of which 2 were waited for; matrix products, arithmetic and copies ran while one was open for 58% of the time, Pallas kernels for 0%

commit v1 on v0

v1 whole, which is shorter than its diff:
```python
import functools

import jax
import jax.numpy as jnp
from jax import lax
from jax.experimental import pallas as pl
from jax.experimental.pallas import tpu as pltpu
from jax.sharding import PartitionSpec as P

F32, BF16 = jnp.float32, jnp.bfloat16
CHUNKS = 4
INNER_TOL = 2e-3
OUTER_TOL = 2e-5
ROWS = 16


def tdot(left, right):
    return lax.dot_general(left, right, (((0,), (0,)), ((), ())), preferred_element_type=F32)


def solve_kernel(width, cols, s_hbm, b_ref, x_ref, sh, sm, sl, stage, stack, r, ri, p, d, q, rr, target, nn, flag, sems):
    blk = stage.shape[1]
    count = width // blk

    def fetch(i, slot):
        return pltpu.make_async_copy(s_hbm.at[pl.ds(i * blk, blk)], stage.at[slot], sems.at[slot])

    fetch(0, 0).start()

    def load(i, carry):
        slot = lax.rem(i, 2)
        fetch(i, slot).wait()

        @pl.when(i + 1 < count)
        def _():
            fetch(i + 1, 1 - slot).start()

        def split(j, c):
            rows = stage[slot, pl.ds(pl.multiple_of(j * ROWS, ROWS), ROWS), :]
            at = pl.ds(pl.multiple_of(i * blk + j * ROWS, ROWS), ROWS)
            high = rows.astype(BF16)
            rest = rows - high.astype(F32)
            mid = rest.astype(BF16)
            sh[at, :] = high
            sm[at, :] = mid
            sl[at, :] = (rest - mid.astype(F32)).astype(BF16)
            return c

        lax.fori_loop(0, blk // ROWS, split, 0)
        return carry

    lax.fori_loop(0, count, load, 0)

    parts = cols // ROWS

    def at(i):
        return slice(i * ROWS, (i + 1) * ROWS)

    def lanes(v):
        return jnp.broadcast_to(v, (ROWS, 128))

    for i in range(parts):
        b = b_ref[at(i), :]
        x_ref[at(i), :] = jnp.zeros_like(b)
        r[at(i), :] = b
        nn[at(i), :] = lanes(jnp.sum(b * b, axis=1, keepdims=True))

    def outer(carry):
        k, _ = carry
        for i in range(parts):
            v = r[at(i), :]
            ri[at(i), :] = v
            p[at(i), :] = v
            d[at(i), :] = jnp.zeros_like(v)
            rr[at(i), :] = nn[at(i), :]
            target[at(i), :] = nn[at(i), :] * (INNER_TOL * INNER_TOL)

        def inner(carry):
            it, _ = carry
            for i in range(parts):
                v = p[at(i), :]
                high = v.astype(BF16)
                stack[at(i), :] = high
                stack[cols + i * ROWS : cols + (i + 1) * ROWS, :] = (v - high.astype(F32)).astype(BF16)
            wide = jnp.dot(stack[: 2 * cols, :], sh[...], preferred_element_type=F32)
            q[...] = wide[:cols] + wide[cols:]

            @pl.when(k >= 2)
            def _():
                q[...] += jnp.dot(stack[:cols, :], sm[...], preferred_element_type=F32)

            worst = jnp.float32(-1.0)
            for i in range(parts):
                v, w = p[at(i), :], q[at(i), :]
                old = rr[at(i), :1]
                pq = jnp.sum(v * w, axis=1, keepdims=True)
                alpha = jnp.where(pq > 0, old / jnp.where(pq > 0, pq, 1.0), 0.0)
                d[at(i), :] += alpha * v
                res = ri[at(i), :] - alpha * w
                ri[at(i), :] = res
                new = jnp.sum(res * res, axis=1, keepdims=True)
                beta = jnp.where(old > 0, new / jnp.where(old > 0, old, 1.0), 0.0)
                p[at(i), :] = res + beta * v
                rr[at(i), :] = lanes(new)
                worst = jnp.maximum(worst, jnp.max(new - target[at(i), :1]))
            return it + 1, worst

        cap = jnp.where(k < 2, 64, 4000)
        lax.while_loop(lambda c: jnp.logical_and(c[0] < cap, c[1] > 0), inner, (jnp.int32(0), jnp.float32(1.0)))

        for i in range(parts):
            v = x_ref[at(i), :] + d[at(i), :]
            d[at(i), :] = v
            high = v.astype(BF16)
            rest = v - high.astype(F32)
            mid = rest.astype(BF16)
            stack[at(i), :] = high
            stack[cols + i * ROWS : cols + (i + 1) * ROWS, :] = mid
            stack[2 * cols + i * ROWS : 2 * cols + (i + 1) * ROWS, :] = (rest - mid.astype(F32)).astype(BF16)
        wide = jnp.dot(stack[...], sh[...], preferred_element_type=F32)
        q[...] = wide[:cols] + wide[cols : 2 * cols] + wide[2 * cols :]
        wide = jnp.dot(stack[: 2 * cols, :], sm[...], preferred_element_type=F32)
        q[...] += wide[:cols] + wide[cols:]
        q[...] += jnp.dot(stack[:cols, :], sl[...], preferred_element_type=F32)
        worst = jnp.float32(-1.0)
        for i in range(parts):
            new = b_ref[at(i), :] - q[at(i), :]
            size = jnp.sum(new * new, axis=1, keepdims=True)
            better = size < nn[at(i), :1]
            x = jnp.where(better, d[at(i), :], x_ref[at(i), :])
            x_ref[at(i), :] = x
            r[at(i), :] = jnp.where(better, new, r[at(i), :])
            kept = jnp.where(better, size, nn[at(i), :1])
            nn[at(i), :] = lanes(kept)
            norm = jnp.sum(x * x, axis=1, keepdims=True)
            worst = jnp.maximum(worst, jnp.max(kept - (OUTER_TOL * OUTER_TOL) * norm))
        return k + 1, worst

    lax.while_loop(lambda c: jnp.logical_and(c[0] < 20, c[1] > 0), outer, (jnp.int32(0), jnp.float32(1.0)))


def solve(system, right):
    width = system.shape[0]
    cols = right.shape[0]
    vec = pltpu.VMEM((cols, width), F32)
    col = pltpu.VMEM((cols, 128), F32)
    piece = pltpu.VMEM((width, width), BF16)

    def body(s_hbm, b_ref, x_ref, sh, sm, sl, stage, stack, r, ri, p, d, q, rr, target, nn, sems):
        solve_kernel(width, cols, s_hbm, b_ref, x_ref, sh, sm, sl, stage, stack, r, ri, p, d, q, rr, target, nn, None, sems)

    return pl.pallas_call(
        body,
        out_shape=jax.ShapeDtypeStruct((cols, width), F32),
        in_specs=[pl.BlockSpec(memory_space=pl.ANY), pl.BlockSpec(memory_space=pltpu.VMEM)],
        out_specs=pl.BlockSpec(memory_space=pltpu.VMEM),
        scratch_shapes=[
            piece, piece, piece,
            pltpu.VMEM((2, 256, width), F32),
            pltpu.VMEM((3 * cols, width), BF16),
            vec, vec, vec, vec, vec,
            col, col, col,
            pltpu.SemaphoreType.DMA((2,)),
        ],
        compiler_params=pltpu.CompilerParams(vmem_limit_bytes=60 << 20),
        name="solve",
    )(system, right)


def local(hidden, token_ids, weights):
    tokens = hidden[0]
    weight = weights[0]
    live = token_ids[0] != 128004
    masked = jnp.where(live[:, None], tokens, 0)
    count, width = masked.shape
    cols = weight.shape[1]
    wide = masked.astype(F32)
    stats = jnp.concatenate([
        jnp.sum(wide * wide, axis=0),
        jnp.full((128,), jnp.sum(live.astype(F32))),
    ]).reshape(1, -1, 128)
    gathered = lax.all_gather(stats, ("expert", "tok"), axis=0, tiled=True)
    experts = lax.axis_size("expert")
    toks = lax.axis_size("tok")
    per_expert = jnp.sum(gathered.reshape(experts, toks, -1), axis=1)
    squares = per_expert[:, :width]
    counts = per_expert[:, width]
    diagonal = jnp.sum(squares / counts[:, None], axis=0)
    scale = 1.0 / jnp.sqrt(diagonal)
    mine = lax.axis_index("expert")
    band = lax.axis_index("tok")
    my_squares = lax.dynamic_index_in_dim(squares, mine, 0, keepdims=False)
    my_count = lax.dynamic_index_in_dim(counts, mine, 0, keepdims=False)

    band_rows = width // toks
    step = count // CHUNKS
    gram = jnp.zeros((band_rows, width), F32)
    projected = jnp.zeros((cols, width), F32)
    for c in range(CHUNKS):
        piece = lax.all_gather(masked[c * step : (c + 1) * step], "tok", axis=0, tiled=True)
        own = lax.dynamic_slice_in_dim(piece, band * band_rows, band_rows, axis=1)
        gram = gram + tdot(own, piece)
        upward = jnp.dot(piece, weight, preferred_element_type=F32).astype(BF16)
        projected = projected + tdot(upward, piece)

    rows = lax.psum(gram / my_count, "expert")
    row_scale = lax.dynamic_slice_in_dim(scale, band * band_rows, band_rows, axis=0)
    at_row = lax.broadcasted_iota(jnp.int32, rows.shape, 0) + band * band_rows
    at_col = lax.broadcasted_iota(jnp.int32, rows.shape, 1)
    rows = jnp.where(at_row == at_col, 1.0, 0.9 * rows * row_scale[:, None] * scale[None, :])
    system = lax.all_gather(rows, "tok", axis=0, tiled=True)

    terms = (0.9 * projected + 0.1 * my_squares[None, :] * weight.T.astype(F32)) / my_count
    right = lax.psum_scatter(terms * scale[None, :], "expert", scatter_dimension=0, tiled=True)
    answer = solve(system, right) * scale[None, :]
    return lax.all_gather(answer, "expert", axis=0, tiled=True).T


def solution(mesh):
    return jax.shard_map(
        local,
        mesh=mesh,
        in_specs=(P("expert", "tok", None), P("expert", "tok"), P("expert", None, "tok")),
        out_specs=P(None, "tok"),
        check_vma=False,
    )
```

time: 1190 us -> 777 us (0.65)
  other arithmetic: 513 us -> 7.74 us
  Pallas kernels: 0 us -> 207 us
  waiting for transfers between devices: 299 us -> 471 us
  matrix products: 218 us -> 59.7 us
  local copies, waits for them, and re-layouts: 87.9 us -> 12.3 us
  blocking collectives: 36 us -> 0 us
  between operations: 26.2 us -> 13.3 us
    another operation x68 -> x0, other arithmetic: 487 us -> none  [the longest x59 321 us: factor_blocks(): factor_block = jnp.linalg.cholesky(corner)]
    all_gather x1 -> x7, waiting for transfers between devices: 0.01 us -> 419 us  [the longest x4 198 us: local(): lax.all_gather(masked[c * step:(c + 1) * step], 'tok', axis=0, tiled=True)]
    psum x2 -> x1, waiting for transfers between devices: 299 us -> 14.3 us  [local(): rows = lax.psum(gram / my_count, 'expert')]
    pallas_call x0 -> x1, Pallas kernels: none -> 207 us  [solve(): pl.pallas_call(body, out_shape=jax.ShapeDtypeStruct((cols, width), F32),...]
    dot_general x24 -> x8, matrix products: 165 us -> 59.7 us  [tdot(): lax.dot_general(left, right, (((0,), (0,)), ((), ())), preferred_element_...]
    another operation x52 -> x0, matrix products: 53.7 us -> none  [the longest x28 30 us: factor_blocks(): jax.scipy.linalg.solve_triangular(factor_block, jnp.eye(block_size, dtype...]
    another operation x69 -> x0, local copies, waits for them, and re-layouts: 49 us -> none  [the longest x53 46.5 us: factor_blocks(): jax.scipy.linalg.solve_triangular(factor_block, jnp.eye(block_size, dtype...]
    reduce_scatter x0 -> x1, waiting for transfers between devices: none -> 36.3 us  [local(): lax.psum_scatter(terms * scale[None, :], 'expert', scatter_dimension=0, t...]
  transfers between devices with their start and end apart: 3 -> 9, of which waited for: 2 -> 9; matrix products, arithmetic and copies ran while one was open for 58% -> 8% of each run, Pallas kernels for 0% -> 0%
where the time goes in v1:
time: 777 us; the launch traced here: 772 us
  waiting for transfers between devices  471 us (61%)
  Pallas kernels  207 us (27%)
  matrix products  59.7 us (8%)
  between operations  13.3 us (2%)
  local copies, waits for them, and re-layouts  12.3 us (2%)
    pallas_call x1, Pallas kernels, solve(): pl.pallas_call(body, out_shape=jax.ShapeDtypeStruct((cols, width), F32),...  207 us
    all_gather x4, waiting for transfers between devices, local(): lax.all_gather(masked[c * step:(c + 1) * step], 'tok', axis=0, tiled=True)  198 us
    all_gather x1, waiting for transfers between devices, local(): system = lax.all_gather(rows, 'tok', axis=0, tiled=True)  115 us
    all_gather x1, waiting for transfers between devices, local(): gathered = lax.all_gather(stats, ('expert', 'tok'), axis=0, tiled=True)  62.3 us
    dot_general x8, matrix products, tdot(): lax.dot_general(left, right, (((0,), (0,)), ((), ())), preferred_element_...  59.7 us
    all_gather x1, waiting for transfers between devices, local(): return lax.all_gather(answer, 'expert', axis=0, tiled=True).T  43.1 us
    reduce_scatter x1, waiting for transfers between devices, local(): lax.psum_scatter(terms * scale[None, :], 'expert', scatter_dimension=0, t...  36.3 us
  transfers between devices with their start and end apart: 9, of which 9 were waited for; matrix products, arithmetic and copies ran while one was open for 8% of the time, Pallas kernels for 0%

profile of v1, /device:TPU:1, one launch (start us, length us, event | category | flops | bytes accessed | tf_op | source)
XLA Modules:
  0.0 771.7 jit_solution(283084503036521239)
XLA Ops:
  6.5 0.0 copy-start
  6.5 0.0 all-gather.16.cloned.1.call-start
  6.5 0.8 compare_reduce_fusion
  7.4 0.6 convert_reduce_fusion
  8.0 1.6 multiply_reduce_fusion
  9.6 1.2 pad_bitcast_fusion
  10.9 0.0 all-gather.16.cloned.1.call-update
  10.9 0.0 all-gather.8.cloned.1.call-start
  10.9 1.0 fusion.43
  11.9 0.0 all-gather.8.cloned.1.call-update
  11.9 0.0 all-gather.10.cloned.1.call-start
  12.0 0.7 all-gather.10.cloned.1.call-update
  12.7 0.0 all-gather.12.cloned.1.call-start
  12.7 0.5 all-gather.12.cloned.1.call-update
  13.2 0.0 all-gather.14.cloned.1.call-start
  13.3 0.5 all-gather.14.cloned.1.call-update
  13.8 0.0 all-reduce.3.cloned.1.call-start
  13.9 0.0 copy-done
  13.9 2.5 copy.10
  16.4 62.3 %all-gather.16.cloned.1.call-done = f32[128,17,128]{2,1,0:T(8,128)} async-done(((f32[1,17,128]{2,1,0:T(8,128)}), f32[128,17,128]{2,1,0:T(8,128)}) %all-gather.16.cloned.1.call-update) | async-done | bytes 1114128 | tf_op jit(solution)/shard_map/all_gather | solution.py:182
  78.7 1.5 reshape.20
  80.3 0.2 reduce_sum.38
  80.4 0.1 slice_reduce_fusion
  80.6 0.1 fusion.44
  80.7 0.6 constant_dynamic-slice_fusion
  81.3 48.0 %all-gather.8.cloned.1.call-done = bf16[1024,2048]{1,0:T(8,128)(2,1)} async-done(((bf16[64,2048]{1,0:T(8,128)(2,1)}), bf16[1024,2048]{1,0:T(8,128)(2,1)}) %all-gather.8.cloned.1.call-update) | async-done | bytes 4194320 | tf_op jit(solution)/shard_map/all_gather | solution.py:200
  129.3 3.0 fusion.37
  132.3 50.2 %all-gather.10.cloned.1.call-done = bf16[1024,2048]{1,0:T(8,128)(2,1)} async-done(((bf16[64,2048]{1,0:T(8,128)(2,1)}), bf16[1024,2048]{1,0:T(8,128)(2,1)}) %all-gather.10.cloned.1.call-update) | async-done | bytes 4194320 | tf_op jit(solution)/shard_map/all_gather | solution.py:200
  182.5 3.0 convolution_add_fusion.2
  185.5 50.0 %all-gather.12.cloned.1.call-done = bf16[1024,2048]{1,0:T(8,128)(2,1)} async-done(((bf16[64,2048]{1,0:T(8,128)(2,1)}), bf16[1024,2048]{1,0:T(8,128)(2,1)}) %all-gather.12.cloned.1.call-update) | async-done | bytes 4194320 | tf_op jit(solution)/shard_map/all_gather | solution.py:200
  235.6 3.0 convolution_add_fusion.1
  238.6 0.0 copy-start.1
  238.6 50.0 %all-gather.14.cloned.1.call-done = bf16[1024,2048]{1,0:T(8,128)(2,1)} async-done(((bf16[64,2048]{1,0:T(8,128)(2,1)}), bf16[1024,2048]{1,0:T(8,128)(2,1)}) %all-gather.14.cloned.1.call-update) | async-done | bytes 4194320 | tf_op jit(solution)/shard_map/all_gather | solution.py:200
  288.7 4.7 fusion.2
  293.3 0.0 all-reduce.3.cloned.1.call-update
  293.4 0.2 reduce-scatter.2.cloned.1.call-start
  293.6 0.0 copy-done.1
  293.6 9.9 %fusion.32 = f32[512,2048]{1,0:T(8,128)} fusion(bf16[1024,2048]{1,0:T(8,128)(2,1)} %all-gather.8.cloned.1.call-done, bf16[1,2048,512]{2,1,0:T(8,128)(2,1)S(1)} %copy-done.1), kind=kOutput, calls=%fused_computation.25 | convolution fusion | flops 4295491584 | bytes 10485760 | tf_op jit(solution)/shard_map/dot_general | solution.py:18
  303.5 10.0 %fusion.29 = f32[512,2048]{1,0:T(8,128)} fusion(bf16[1024,2048]{1,0:T(8,128)(2,1)} %all-gather.10.cloned.1.call-done, bf16[1,2048,512]{2,1,0:T(8,128)(2,1)S(1)} %copy-done.1), kind=kOutput, calls=%fused_computation.24 | convolution fusion | flops 4295491584 | bytes 10485760 | tf_op jit(solution)/shard_map/dot_general | solution.py:18
  313.5 10.1 %fusion.26 = f32[512,2048]{1,0:T(8,128)} fusion(bf16[1024,2048]{1,0:T(8,128)(2,1)} %all-gather.12.cloned.1.call-done, bf16[1,2048,512]{2,1,0:T(8,128)(2,1)S(1)} %copy-done.1), kind=kOutput, calls=%fused_computation.23 | convolution fusion | flops 4295491584 | bytes 10485760 | tf_op jit(solution)/shard_map/dot_general | solution.py:18
  323.5 15.9 %fusion.1 = f32[512,2048]{1,0:T(8,128)} fusion(f32[512,2048]{1,0:T(8,128)} %fusion.26, f32[512,2048]{1,0:T(8,128)} %fusion.32, f32[512,2048]{1,0:T(8,128)} %fusion.29, bf16[1024,2048]{1,0:T(8,128)(2,1)} %all-gather.14.cloned.1.call-done, bf16[1,2048,512]{1,2,0:T(8,128)(2,1)} %copy.10, f32[2048]{0:T(1024)S(1)} %sqrt.3, f32[]{:T(128)} %bitcast.2, ...), kind=kOutput, calls=%fused_computation.2 | convolution fusion | flops 4304928768 | bytes 25182212 | tf_op jit(solution)/shard_map/dot_general | solution.py:18
  339.5 0.0 reduce-scatter.2.cloned.1.call-update
  339.5 0.0 all-gather.18.cloned.1.call-start
  339.6 0.1 dynamic-slice_multiply_fusion.1
  339.7 14.3 %all-reduce.3.cloned.1.call-done = f32[128,2048]{1,0:T(8,128)} async-done(((f32[128,2048]{1,0:T(8,128)}), f32[128,2048]{1,0:T(8,128)}) %all-reduce.3.cloned.1.call-update) | async-done | bytes 1048592 | tf_op jit(solution)/shard_map/psum | solution.py:206
  354.0 2.4 multiply_select_fusion
  356.4 0.0 all-gather.18.cloned.1.call-update
  356.4 0.0 all-gather.20.cloned.1.call-start
  356.5 36.3 %reduce-scatter.2.cloned.1.call-done.b_ref = f32[64,2048]{1,0:T(8,128)} async-done(((f32[512,2048]{1,0:T(8,128)}), f32[64,2048]{1,0:T(8,128)}) %reduce-scatter.2.cloned.1.call-update) | async-done | bytes 524304 | tf_op jit(solution)/shard_map/reduce_scatter | solution.py:214
  392.8 115.1 %all-gather.18.cloned.1.call-done.s_hbm = f32[2048,2048]{1,0:T(8,128)} async-done(((f32[128,2048]{1,0:T(8,128)}), f32[2048,2048]{1,0:T(8,128)}) %all-gather.18.cloned.1.call-update) | async-done | bytes 16777232 | tf_op jit(solution)/shard_map/all_gather | solution.py:211
  507.9 206.8 %solve.1 = f32[64,2048]{1,0:T(8,128)} custom-call(f32[2048,2048]{1,0:T(8,128)} %all-gather.18.cloned.1.call-done.s_hbm, f32[64,2048]{1,0:T(8,128)} %reduce-scatter.2.cloned.1.call-done.b_ref), custom_call_target="tpu_custom_call" | custom-call | tf_op jit(solution)/shard_map/solve/pallas_call | solution.py:152
  714.7 1.9 broadcast_multiply_fusion
  716.6 0.0 all-gather.20.cloned.1.call-update
  716.6 43.1 %all-gather.20.cloned.1.call-done = f32[512,2048]{1,0:T(8,128)} async-done(((f32[64,2048]{1,0:T(8,128)}), f32[512,2048]{1,0:T(8,128)}) %all-gather.20.cloned.1.call-update) | async-done | bytes 4194320 | tf_op jit(solution)/shard_map/all_gather | solution.py:216
  759.8 5.3 copy.11
  (3 shorter events, 0.0 us)
Async XLA Ops:
  6.5 7.4 copy-start
  6.5 72.2 %all-gather.16.cloned.1.call-start = ((), (), s32[]{:S(2)}) async-start(), calls=%async_computation.5 | async-start | bytes 1585152 | tf_op jit(solution)/shard_map/all_gather | solution.py:182
  10.9 118.4 %all-gather.8.cloned.1.call-start = ((), (), s32[]{:S(2)}) async-start(), calls=%async_computation.1 | async-start | bytes 4456448 | tf_op jit(solution)/shard_map/all_gather | solution.py:200
  11.9 170.6 %all-gather.10.cloned.1.call-start = ((), (), s32[]{:S(2)}) async-start(), calls=%async_computation.2 | async-start | bytes 4456448 | tf_op jit(solution)/shard_map/all_gather | solution.py:200
  12.7 222.9 %all-gather.12.cloned.1.call-start = ((), (), s32[]{:S(2)}) async-start(), calls=%async_computation.3 | async-start | bytes 4456448 | tf_op jit(solution)/shard_map/all_gather | solution.py:200
  13.2 275.4 %all-gather.14.cloned.1.call-start = ((), (), s32[]{:S(2)}) async-start(), calls=%async_computation.4 | async-start | bytes 4456448 | tf_op jit(solution)/shard_map/all_gather | solution.py:200
  13.8 340.1 %all-reduce.3.cloned.1.call-start = ((), (), s32[]{:S(2)}) async-start(), calls=%async_computation.6 | async-start | bytes 2097152 | tf_op jit(solution)/shard_map/psum | solution.py:206
  238.6 55.0 %copy-start.1 = (bf16[1,2048,512]{2,1,0:T(8,128)(2,1)S(1)}, bf16[1,2048,512]{2,1,0:T(8,128)(2,1)}, u32[]{:S(2)}) copy-start(bf16[1,2048,512]{2,1,0:T(8,128)(2,1)} %param.5) | copy-start | bytes 6291460
  293.4 99.5 %reduce-scatter.2.cloned.1.call-start = ((), (), s32[]{:S(2)}) async-start(), calls=%async_computation.8 | async-start | bytes 4718592 | tf_op jit(solution)/shard_map/reduce_scatter | solution.py:214
  339.5 168.4 %all-gather.18.cloned.1.call-start = ((), (), s32[]{:S(2)}) async-start(), calls=%async_computation.7 | async-start | bytes 17825792 | tf_op jit(solution)/shard_map/all_gather | solution.py:211
  356.4 403.3 %all-gather.20.cloned.1.call-start = ((), (), s32[]{:S(2)}) async-start(), calls=%async_computation.9 | async-start | bytes 4718592 | tf_op jit(solution)/shard_map/all_gather | solution.py:216
Sparse Core Ops, SparseCore 0:
  11.0 67.6 all-gather.15
  80.9 48.3 all-gather.7
  131.4 51.0 all-gather.9
  184.5 51.0 all-gather.11
  237.6 51.0 all-gather.13
  293.5 60.4 all-reduce.2
  356.4 36.3 reduce-scatter.1
  395.0 112.9 all-gather.17
  716.8 42.9 all-gather.19

commit v2 on v1

--- a/solution.py
+++ b/solution.py
@@ -8,17 +8,435 @@
 from jax.sharding import PartitionSpec as P
 
 F32, BF16 = jnp.float32, jnp.bfloat16
-CHUNKS = 4
+MESH = pl.DeviceIdType.MESH
+SIDE = 4
 INNER_TOL = 2e-3
 OUTER_TOL = 2e-5
 ROWS = 16
 
 
-def tdot(left, right):
-    return lax.dot_general(left, right, (((0,), (0,)), ((), ())), preferred_element_type=F32)
-
-
-def solve_kernel(width, cols, s_hbm, b_ref, x_ref, sh, sm, sl, stage, stack, r, ri, p, d, q, rr, target, nn, flag, sems):
+def near(i, step):
+    return (i + step + SIDE) % SIDE
+
+
+def remote(sems, index, source, target, device):
+    send, recv = sems
+    return pltpu.make_async_remote_copy(
+        src_ref=source, dst_ref=target, send_sem=send.at[index], recv_sem=recv.at[index],
+        device_id=device, device_id_type=MESH,
+    )
+
+
+def meet(devices):
+    barrier = pltpu.get_barrier_semaphore()
+    for device in devices:
+        pl.semaphore_signal(barrier, inc=1, device_id=device, device_id_type=MESH)
+    pl.semaphore_wait(barrier, len(devices))
+
+
+def gather_kernel(toks, x_hbm, ids_ref, w_ref, terms_ref, gram_ref, X, cat, acc, wt, stat, stats, send, recv, own, stat_send, stat_recv):
+    t = lax.axis_index("tok")
+    z, x = t // SIDE, t % SIDE
+    width, cols = w_ref.shape
+    band = width // toks
+    half = x_hbm.shape[0] // 2
+
+    def tok(zz, xx):
+        return {"tok": zz * SIDE + xx}
+
+    meet([{"tok": (t + k) % toks} for k in range(1, toks)])
+    mine = (X.at[z, x], X.at[SIDE + x, z])
+    loads = [pltpu.make_async_copy(x_hbm.at[pl.ds(k * half, half)], mine[k], own.at[k]) for k in range(2)]
+    for load in loads:
+        load.start()
+
+    rc = functools.partial(remote, (send, recv))
+
+    def steps(base, block_of, part, to, here):
+        up, down = near(here, 1), near(here, -1)
+        first = [
+            rc(base, block_of(here), block_of(here), to(up)),
+            rc(base + 1, block_of(here), block_of(here), to(down)),
+        ]
+        onward = [
+            rc(base + 2, part(down, 0), part(down, 0), to(up)),
+            rc(base + 3, part(up, 1), part(up, 1), to(down)),
+        ]
+        return first, onward
+
+    a_first, a_onward = steps(
+        0, lambda i: X.at[z, i], lambda i, h: X.at[z, i, pl.ds(h * (half // 2), half // 2)], lambda i: tok(z, i), x)
+    b_first, b_onward = steps(
+        4, lambda i: X.at[SIDE + x, i], lambda i, h: X.at[SIDE + x, i, pl.ds(h * (half // 2), half // 2)], lambda i: tok(i, x), z)
+
+    loads[0].wait()
+    for copy in a_first:
+        copy.start()
+    loads[1].wait()
+    for copy in b_first:
+        copy.start()
+
+    def clear(i, c):
+        at = pl.ds(pl.multiple_of(i * ROWS, ROWS), ROWS)
+        acc[at, :] = jnp.zeros((ROWS, width), F32)
+        return c
+
+    lax.fori_loop(0, acc.shape[0] // ROWS, clear, 0)
+
+    live = jnp.sum(jnp.where(ids_ref[...] != 128004, 1.0, 0.0), axis=(0, 1), keepdims=True)
+
+    def square(i, total):
+        at = pl.ds(pl.multiple_of(i * ROWS, ROWS), ROWS)
+        a = X[z, x, at, :].astype(F32)
+        b = X[SIDE + x, z, at, :].astype(F32)
+        return total + jnp.sum(a * a + b * b, axis=0, keepdims=True)
+
+    stat[:, :width] = lax.fori_loop(0, half // ROWS, square, jnp.zeros((1, width), F32))
+    stat[:, width:] = jnp.broadcast_to(live, (1, 128))
+
+    def turn(i, c):
+        at = pl.ds(pl.multiple_of(i * 256, 256), 256)
+        wt[:, at] = w_ref[at, :].T
+        return c
+
+    lax.fori_loop(0, width // 256, turn, 0)
+
+    for first, onward in ((a_first, a_onward), (b_first, b_onward)):
+        for got, copy in zip(first, onward):
+            got.wait_recv()
+            copy.start()
+
+    def share(k):
+        return pltpu.make_async_remote_copy(
+            src_ref=stat, dst_ref=stats.at[k], send_sem=stat_send.at[k], recv_sem=stat_recv.at[k],
+            device_id={"tok": (t + k) % toks}, device_id_type=MESH,
+        )
+
+    for copy in a_onward + b_onward:
+        copy.wait_recv()
+
+    def group(base, g_of, to, here):
+        up, down = near(here, 1), near(here, -1)
+
+        def part(i, h):
+            return X.at[g_of(i), pl.ds(2 * h, 2)]
+
+        first = {}
+        for h in range(2):
+            first["up", h] = rc(base + h, part(here, h), part(here, h), to(up))
+            first["down", h] = rc(base + 2 + h, part(here, h), part(here, h), to(down))
+        onward = [
+            rc(base + 4, part(down, 0), part(down, 0), to(up)),
+            rc(base + 5, part(up, 1), part(up, 1), to(down)),
+        ]
+        return first, onward
+
+    a_near, a_far = group(8, lambda i: i, lambda i: tok(i, x), z)
+    b_near, b_far = group(14, lambda i: SIDE + i, lambda i: tok(z, i), x)
+    for h in range(2):
+        for copies in (a_near, b_near):
+            copies["up", h].start()
+            copies["down", 1 - h].start()
+
+    lax.fori_loop(1, toks, lambda k, c: (share(k).start(), c)[1], 0)
+
+    arrivals = {}
+    for k, (first, far) in enumerate(((a_near, a_far), (b_near, b_far))):
+        arrivals[4 + 2 * k] = (first["up", 0], far[0])
+        arrivals[5 + 2 * k] = (first["down", 1], far[1])
+        arrivals[8 + 2 * k] = (first["up", 1], None)
+        arrivals[9 + 2 * k] = (first["down", 0], None)
+        arrivals[12 + 2 * k] = (far[0], None)
+        arrivals[13 + 2 * k] = (far[1], None)
+
+    pair = 2 * half
+
+    def step(s, c):
+        @pl.when(s == 4)
+        def _():
+            for at in range(4, 8):
+                got, copy = arrivals[at]
+                got.wait_recv()
+                copy.start()
+
+        for at in range(8, 16):
+            @pl.when(s == at)
+            def _(at=at):
+                arrivals[at][0].wait_recv()
+
+        q, m = s // 4, s % 4
+        kind, a = m // 2, m % 2
+        close = (q % 3 + 1) // 2
+        off = close * (3 - 2 * a) + 2 * (q // 3)
+        h = a + (q // 2) * (1 - q // 3) * (1 - 2 * a)
+        here = z * (1 - kind) + x * kind
+        g = kind * SIDE + (here + off) % SIDE
+        block = X.at[g, pl.ds(2 * h, 2)]
+        rows = block[...].reshape(pair, width)
+        upward = jnp.dot(rows, w_ref[...], preferred_element_type=F32).astype(BF16)
+        cat[:cols, :] = upward.T
+        cat[cols:, :] = block[:, :, pl.ds(pl.multiple_of(t * band, band), band)].reshape(pair, band).T
+
+        def tile(n, c):
+            at = pl.ds(pl.multiple_of(n * 512, 512), 512)
+            acc[:, at] += jnp.dot(cat[...], block[:, :, at].reshape(pair, 512), preferred_element_type=F32)
+            return c
+
+        lax.fori_loop(0, width // 512, tile, 0)
+        return c
+
+    lax.fori_loop(0, 16, step, 0)
+
+    lax.fori_loop(1, toks, lambda k, c: (share(k).wait_recv(), c)[1], 0)
+    total = stat[...]
+    for k in range(1, toks):
+        total = total + stats[k]
+    inverse = 1.0 / total[:, width : width + 1]
+    squares = total[:, :width] * (0.1 * inverse)
+
+    def finish(i, c):
+        at = pl.ds(pl.multiple_of(i * ROWS, ROWS), ROWS)
+        terms_ref[at, :] = acc[at, :] * (0.9 * inverse) + squares * wt[at, :].astype(F32)
+        return c
+
+    lax.fori_loop(0, cols // ROWS, finish, 0)
+
+    def finish_gram(i, c):
+        at = pl.ds(pl.multiple_of(i * ROWS, ROWS), ROWS)
+        gram_ref[at, :] = acc[pl.ds(pl.multiple_of(cols + i * ROWS, ROWS), ROWS), :] * inverse
+        return c
+
+    lax.fori_loop(0, band // ROWS, finish_gram, 0)
+
+    for copy in a_first + b_first + a_onward + b_onward + list(a_near.values()) + list(b_near.values()) + a_far + b_far:
+        copy.wait_send()
+    lax.fori_loop(1, toks, lambda k, c: (share(k).wait_send(), c)[1], 0)
+
+
+def gather(masked, ids, weight, toks):
+    count, width = masked.shape
+    cols = weight.shape[1]
+    band = width // toks
+    half = count // 2
+    vmem = pl.BlockSpec(memory_space=pltpu.VMEM)
+    return pl.pallas_call(
+        functools.partial(gather_kernel, toks),
+        out_shape=(jax.ShapeDtypeStruct((cols, width), F32), jax.ShapeDtypeStruct((band, width), F32)),
+        in_specs=[pl.BlockSpec(memory_space=pl.ANY), vmem, vmem],
+        out_specs=(vmem, vmem),
+        scratch_shapes=[
+            pltpu.VMEM((2 * SIDE, SIDE, half, width), BF16),
+            pltpu.VMEM((cols + band, 2 * half), BF16),
+            pltpu.VMEM((cols + band, width), F32),
+            pltpu.VMEM((cols, width), BF16),
+            pltpu.VMEM((1, width + 128), F32),
+            pltpu.VMEM((toks, 1, width + 128), F32),
+            pltpu.SemaphoreType.DMA((20,)),
+            pltpu.SemaphoreType.DMA((20,)),
+            pltpu.SemaphoreType.DMA((2,)),
+            pltpu.SemaphoreType.DMA((toks,)),
+            pltpu.SemaphoreType.DMA((toks,)),
+        ],
+        compiler_params=pltpu.CompilerParams(collective_id=0, has_side_effects=True, vmem_limit_bytes=60 << 20),
+        name="gather",
+    )(masked, ids, weight)
+
+
+def combine_kernel(g_ref, terms_ref, s, b_ref, pg, hg, rg, sg, pt, ht, far, close, send, recv, own):
+    e, t = lax.axis_index("expert"), lax.axis_index("tok")
+    y, c = e // 2, e % 2
+    z, x = t // SIDE, t % SIDE
+    rc = functools.partial(remote, (send, recv))
+
+    def tok(zz, xx):
+        return {"tok": zz * SIDE + xx}
+
+    def chip(yy):
+        return {"expert": yy * 2 + c}
+
+    partner = {"expert": e + 1 - 2 * c}
+    up, down, across = near(y, 1), near(y, -1), near(y, 2)
+    meet([partner, chip(up), chip(down), chip(across), tok(near(z, 1), x), tok(near(z, -1), x), tok(z, near(x, 1)), tok(z, near(x, -1))])
+
+    swap_g = rc(0, g_ref.at[1 - c], pg, partner)
+    swap_t = rc(1, terms_ref.at[:, 1 - c], pt, partner)
+    swap_g.start()
+    swap_t.start()
+
+    swap_g.wait_recv()
+    for k in range(4):
+        hg[k] = g_ref[c, k] + pg[k]
+    scatter = [rc(1 + k, hg.at[near(y, k)], rg.at[k - 1], chip(near(y, k))) for k in range(1, 4)]
+    for copy in scatter:
+        copy.start()
+    for copy in scatter:
+        copy.wait_recv()
+    sg[...] = hg[y] + rg[0] + rg[1] + rg[2]
+    rows = s.at[z, x, c, y // 2, pl.ds((y % 2) * 16, 16)]
+    keep = pltpu.make_async_copy(sg, rows, own.at[0])
+    keep.start()
+    spread = [rc(4 + k, sg, rows, chip(near(y, k))) for k in range(1, 4)]
+    for copy in spread:
+        copy.start()
+
+    swap_t.wait_recv()
+    for k in range(4):
+        ht[k] = terms_ref[k, c] + pt[k]
+    first_t = [
+        rc(8, ht.at[across, pl.ds(0, 32)], far.at[0], chip(up)),
+        rc(9, ht.at[across, pl.ds(32, 32)], far.at[1], chip(down)),
+    ]
+    for copy in first_t:
+        copy.start()
+
+    keep.wait()
+    for copy in spread:
+        copy.wait_recv()
+
+    def stage(base, block, part, to, here):
+        above, below = near(here, 1), near(here, -1)
+        first = [rc(base, block(here), block(here), to(above)), rc(base + 1, block(here), block(here), to(below))]
+        onward = [rc(base + 2, part(below, 0), part(below, 0), to(above)), rc(base + 3, part(above, 1), part(above, 1), to(below))]
+        return first, onward
+
+    a_first, a_onward = stage(10, lambda i: s.at[z, i, c, 0], lambda i, h: s.at[z, i, c, 0, pl.ds(16 * h, 16)], lambda i: tok(z, i), x)
+    b_first, b_onward = stage(14, lambda i: s.at[i, x, c, 1], lambda i, h: s.at[i, x, c, 1, pl.ds(16 * h, 16)], lambda i: tok(i, x), z)
+    for copy in a_first + b_first:
+        copy.start()
+
+    first_t[0].wait_recv()
+    ht[up, :32] = ht[up, :32] + far[0]
+    first_t[1].wait_recv()
+    ht[down, 32:] = ht[down, 32:] + far[1]
+
+    for got, copy in zip(a_first + b_first, a_onward + b_onward):
+        got.wait_recv()
+        copy.start()
+
+    second_t = [rc(18, ht.at[up], close.at[0], chip(up)), rc(19, ht.at[down], close.at[1], chip(down))]
+    for copy in second_t:
+        copy.start()
+
+    for copy in a_onward + b_onward:
+        copy.wait_recv()
+
+    a_near, a_far = stage(20, lambda i: s.at[i, :, c, 0], lambda i, h: s.at[i, pl.ds(2 * h, 2), c, 0], lambda i: tok(i, x), z)
+    b_near, b_far = stage(24, lambda i: s.at[:, i, c, 1], lambda i, h: s.at[pl.ds(2 * h, 2), i, c, 1], lambda i: tok(z, i), x)
+    for copy in a_near + b_near:
+        copy.start()
+
+    def pair(index, block):
+        copy = rc(28 + index, block, block, partner)
+        copy.start()
+        return copy
+
+    pairs = [pair(0, s.at[z, :, c, 0]), pair(1, s.at[:, x, c, 1])]
+
+    for copy in second_t:
+        copy.wait_recv()
+    b_ref[...] = ht[y] + close[0] + close[1]
+
+    for got, copy in zip(a_near + b_near, a_far + b_far):
+        got.wait_recv()
+        copy.start()
+    pairs += [pair(2, s.at[near(z, -1), :, c, 0]), pair(3, s.at[near(z, 1), :, c, 0])]
+    pairs += [pair(4, s.at[:, near(x, -1), c, 1]), pair(5, s.at[:, near(x, 1), c, 1])]
+    for copy in a_far + b_far:
+        copy.wait_recv()
+    pairs += [pair(6, s.at[near(z, 2), :, c, 0]), pair(7, s.at[:, near(x, 2), c, 1])]
+    for copy in pairs:
+        copy.wait_recv()
+    for copy in [swap_g, swap_t] + scatter + spread + first_t + second_t + a_first + b_first + a_onward + b_onward + a_near + b_near + a_far + b_far + pairs:
+        copy.wait_send()
+
+
+def combine(gram, terms):
+    band, width = gram.shape
+    cols = terms.shape[0]
+    part, share = band // 8, cols // 8
+    vmem = pl.BlockSpec(memory_space=pltpu.VMEM)
+    system, right = pl.pallas_call(
+        combine_kernel,
+        out_shape=(
+            jax.ShapeDtypeStruct((SIDE, SIDE, 2, 2, 2 * part, width), F32),
+            jax.ShapeDtypeStruct((share, width), F32),
+        ),
+        in_specs=[vmem, vmem],
+        out_specs=(pl.BlockSpec(memory_space=pl.ANY), vmem),
+        scratch_shapes=[
+            pltpu.VMEM((4, part, width), F32),
+            pltpu.VMEM((4, part, width), F32),
+            pltpu.VMEM((3, part, width), F32),
+            pltpu.VMEM((part, width), F32),
+            pltpu.VMEM((4, share, width), F32),
+            pltpu.VMEM((4, share, width), F32),
+            pltpu.VMEM((2, share // 2, width), F32),
+            pltpu.VMEM((2, share, width), F32),
+            pltpu.SemaphoreType.DMA((36,)),
+            pltpu.SemaphoreType.DMA((36,)),
+            pltpu.SemaphoreType.DMA((1,)),
+        ],
+        compiler_params=pltpu.CompilerParams(collective_id=1, has_side_effects=True, vmem_limit_bytes=60 << 20),
+        name="combine",
+    )(gram.reshape(2, 4, part, width), terms.reshape(4, 2, share, width))
+    return system.reshape(width, width), right
+
+
+def spread_kernel(a_ref, out, send, recv, own):
+    e = lax.axis_index("expert")
+    y, c = e // 2, e % 2
+    share = a_ref.shape[0]
+    rc = functools.partial(remote, (send, recv))
+
+    def chip(yy):
+        return {"expert": yy * 2 + c}
+
+    partner = {"expert": e + 1 - 2 * c}
+    up, down, across = near(y, 1), near(y, -1), near(y, 2)
+    meet([partner, chip(up), chip(down)])
+    half = share // 2
+    first = [rc(0, a_ref, out.at[y, c], chip(up)), rc(1, a_ref, out.at[y, c], chip(down))]
+    pairs = [rc(2, a_ref, out.at[y, c], partner)]
+    for copy in first + pairs:
+        copy.start()
+    keep = pltpu.make_async_copy(a_ref, out.at[y, c], own.at[0])
+    keep.start()
+    lower, upper = out.at[down, c, pl.ds(0, half)], out.at[up, c, pl.ds(half, half)]
+    onward = [rc(3, lower, lower, chip(up)), rc(4, upper, upper, chip(down))]
+    for k, (got, copy, at) in enumerate(zip(first, onward, (down, up))):
+        got.wait_recv()
+        copy.start()
+        forward = rc(5 + k, out.at[at, c], out.at[at, c], partner)
+        forward.start()
+        pairs.append(forward)
+    for k, copy in enumerate(onward):
+        copy.wait_recv()
+        part = out.at[across, c, pl.ds(half * k, half)]
+        forward = rc(7 + k, part, part, partner)
+        forward.start()
+        pairs.append(forward)
+    keep.wait()
+    for copy in pairs:
+        copy.wait_recv()
+    for copy in first + onward + pairs:
+        copy.wait_send()
+
+
+def spread(answer):
+    share, width = answer.shape
+    out = pl.pallas_call(
+        spread_kernel,
+        out_shape=jax.ShapeDtypeStruct((4, 2, share, width), F32),
+        in_specs=[pl.BlockSpec(memory_space=pltpu.VMEM)],
+        out_specs=pl.BlockSpec(memory_space=pl.ANY),
+        scratch_shapes=[pltpu.SemaphoreType.DMA((9,)), pltpu.SemaphoreType.DMA((9,)), pltpu.SemaphoreType.DMA((1,))],
+        compiler_params=pltpu.CompilerParams(collective_id=2, has_side_effects=True),
+        name="spread",
+    )(answer)
+    return out.reshape(8 * share, width)
+
+
+def solve_kernel(width, cols, s_hbm, b_in, x_ref, sh, sm, sl, stage, diag, srow, scol, b_ref, stack, r, ri, p, d, q, rr, target, nn, sems, dsems):
     blk = stage.shape[1]
     count = width // blk
 
@@ -26,6 +444,20 @@
         return pltpu.make_async_copy(s_hbm.at[pl.ds(i * blk, blk)], stage.at[slot], sems.at[slot])
 
     fetch(0, 0).start()
+
+    corners = [
+        pltpu.make_async_copy(s_hbm.at[pl.ds(k * 128, 128), pl.ds(k * 128, 128)], diag.at[k], dsems.at[k])
+        for k in range(width // 128)
+    ]
+    for corner in corners:
+        corner.start()
+    eye = lax.broadcasted_iota(jnp.int32, (128, 128), 0) == lax.broadcasted_iota(jnp.int32, (128, 128), 1)
+    for k, corner in enumerate(corners):
+        corner.wait()
+        only = jnp.where(eye, diag[k], 0.0)
+        srow[:, k * 128 : (k + 1) * 128] = 1.0 / jnp.sqrt(jnp.sum(only, axis=0, keepdims=True))
+        scol[k * 128 : (k + 1) * 128, :] = jnp.broadcast_to(
+            1.0 / jnp.sqrt(jnp.sum(only, axis=1, keepdims=True)), (128, 128))
 
     def load(i, carry):
         slot = lax.rem(i, 2)
@@ -38,6 +470,9 @@
         def split(j, c):
             rows = stage[slot, pl.ds(pl.multiple_of(j * ROWS, ROWS), ROWS), :]
             at = pl.ds(pl.multiple_of(i * blk + j * ROWS, ROWS), ROWS)
+            row = lax.broadcasted_iota(jnp.int32, rows.shape, 0) + (i * blk + j * ROWS)
+            factor = jnp.where(row == lax.broadcasted_iota(jnp.int32, rows.shape, 1), 1.0, 0.9)
+            rows = rows * factor * srow[...] * scol[at, :1]
             high = rows.astype(BF16)
             rest = rows - high.astype(F32)
             mid = rest.astype(BF16)
@@ -60,7 +495,8 @@
         return jnp.broadcast_to(v, (ROWS, 128))
 
     for i in range(parts):
-        b = b_ref[at(i), :]
+        b = b_in[at(i), :] * srow[...]
+        b_ref[at(i), :] = b
         x_ref[at(i), :] = jnp.zeros_like(b)
         r[at(i), :] = b
         nn[at(i), :] = lanes(jnp.sum(b * b, axis=1, keepdims=True))
@@ -137,6 +573,8 @@
         return k + 1, worst
 
     lax.while_loop(lambda c: jnp.logical_and(c[0] < 20, c[1] > 0), outer, (jnp.int32(0), jnp.float32(1.0)))
+    for i in range(parts):
+        x_ref[at(i), :] = x_ref[at(i), :] * srow[...]
 
 
 def solve(system, right):
@@ -146,21 +584,23 @@
     col = pltpu.VMEM((cols, 128), F32)
     piece = pltpu.VMEM((width, width), BF16)
 
-    def body(s_hbm, b_ref, x_ref, sh, sm, sl, stage, stack, r, ri, p, d, q, rr, target, nn, sems):
-        solve_kernel(width, cols, s_hbm, b_ref, x_ref, sh, sm, sl, stage, stack, r, ri, p, d, q, rr, target, nn, None, sems)
-
     return pl.pallas_call(
-        body,
+        functools.partial(solve_kernel, width, cols),
         out_shape=jax.ShapeDtypeStruct((cols, width), F32),
         in_specs=[pl.BlockSpec(memory_space=pl.ANY), pl.BlockSpec(memory_space=pltpu.VMEM)],
         out_specs=pl.BlockSpec(memory_space=pltpu.VMEM),
         scratch_shapes=[
             piece, piece, piece,
             pltpu.VMEM((2, 256, width), F32),
+            pltpu.VMEM((width // 128, 128, 128), F32),
+            pltpu.VMEM((1, width), F32),
+            pltpu.VMEM((width, 128), F32),
+            vec,
             pltpu.VMEM((3 * cols, width), BF16),
             vec, vec, vec, vec, vec,
             col, col, col,
             pltpu.SemaphoreType.DMA((2,)),
+            pltpu.SemaphoreType.DMA((width // 128,)),
         ],
         compiler_params=pltpu.CompilerParams(vmem_limit_bytes=60 << 20),
         name="solve",
@@ -168,52 +608,11 @@
 
 
 def local(hidden, token_ids, weights):
-    tokens = hidden[0]
-    weight = weights[0]
     live = token_ids[0] != 128004
-    masked = jnp.where(live[:, None], tokens, 0)
-    count, width = masked.shape
-    cols = weight.shape[1]
-    wide = masked.astype(F32)
-    stats = jnp.concatenate([
-        jnp.sum(wide * wide, axis=0),
-        jnp.full((128,), jnp.sum(live.astype(F32))),
-    ]).reshape(1, -1, 128)
-    gathered = lax.all_gather(stats, ("expert", "tok"), axis=0, tiled=True)
-    experts = lax.axis_size("expert")
-    toks = lax.axis_size("tok")
-    per_expert = jnp.sum(gathered.reshape(experts, toks, -1), axis=1)
-    squares = per_expert[:, :width]
-    counts = per_expert[:, width]
-    diagonal = jnp.sum(squares / counts[:, None], axis=0)
-    scale = 1.0 / jnp.sqrt(diagonal)
-    mine = lax.axis_index("expert")
-    band = lax.axis_index("tok")
-    my_squares = lax.dynamic_index_in_dim(squares, mine, 0, keepdims=False)
-    my_count = lax.dynamic_index_in_dim(counts, mine, 0, keepdims=False)
-
-    band_rows = width // toks
-    step = count // CHUNKS
-    gram = jnp.zeros((band_rows, width), F32)
-    projected = jnp.zeros((cols, width), F32)
-    for c in range(CHUNKS):
-        piece = lax.all_gather(masked[c * step : (c + 1) * step], "tok", axis=0, tiled=True)
-        own = lax.dynamic_slice_in_dim(piece, band * band_rows, band_rows, axis=1)
-        gram = gram + tdot(own, piece)
-        upward = jnp.dot(piece, weight, preferred_element_type=F32).astype(BF16)
-        projected = projected + tdot(upward, piece)
-
-    rows = lax.psum(gram / my_count, "expert")
-    row_scale = lax.dynamic_slice_in_dim(scale, band * band_rows, band_rows, axis=0)
-    at_row = lax.broadcasted_iota(jnp.int32, rows.shape, 0) + band * band_rows
-    at_col = lax.broadcasted_iota(jnp.int32, rows.shape, 1)
-    rows = jnp.where(at_row == at_col, 1.0, 0.9 * rows * row_scale[:, None] * scale[None, :])
-    system = lax.all_gather(rows, "tok", axis=0, tiled=True)
-
-    terms = (0.9 * projected + 0.1 * my_squares[None, :] * weight.T.astype(F32)) / my_count
-    right = lax.psum_scatter(terms * scale[None, :], "expert", scatter_dimension=0, tiled=True)
-    answer = solve(system, right) * scale[None, :]
-    return lax.all_gather(answer, "expert", axis=0, tiled=True).T
+    masked = jnp.where(live[:, None], hidden[0], 0)
+    terms, gram = gather(masked, token_ids.reshape(-1, 128), weights[0], lax.axis_size("tok"))
+    system, right = combine(gram, terms)
+    return spread(solve(system, right)).T
 
 
 def solution(mesh):

time: 777 us -> 449 us (0.58)
  waiting for transfers between devices: 471 us -> 0 us
  Pallas kernels: 207 us -> 440 us
  matrix products: 59.7 us -> 0 us
  between operations: 13.3 us -> 0.03 us
    all_gather x7 -> x0, waiting for transfers between devices: 419 us -> none  [the longest x4 198 us: local(): lax.all_gather(masked[c * step:(c + 1) * step], 'tok', axis=0, tiled=True)]
    pallas_call x1 -> x4, Pallas kernels: 207 us -> 440 us  [the longest x1 208 us: solve(): pl.pallas_call(functools.partial(solve_kernel, width, cols), out_shape=ja...]
    dot_general x8 -> x0, matrix products: 59.7 us -> none  [tdot(): lax.dot_general(left, right, (((0,), (0,)), ((), ())), preferred_element_...]
    reduce_scatter x1 -> x0, waiting for transfers between devices: 36.3 us -> none  [local(): lax.psum_scatter(terms * scale[None, :], 'expert', scatter_dimension=0, t...]
    psum x1 -> x0, waiting for transfers between devices: 14.3 us -> none  [local(): rows = lax.psum(gram / my_count, 'expert')]
  transfers between devices with their start and end apart: 9 -> 0, of which waited for: 9 -> 0; matrix products, arithmetic and copies ran while one was open for 8% -> 0% of each run, Pallas kernels for 0% -> 0%
where the time goes in v2:
time: 449 us; the launch traced here: 448 us
  Pallas kernels  440 us (98%)
  local copies, waits for them, and re-layouts  5.35 us (1%)
    pallas_call x1, Pallas kernels, solve(): pl.pallas_call(functools.partial(solve_kernel, width, cols), out_shape=ja...  208 us
    pallas_call x1, Pallas kernels, gather(): pl.pallas_call(functools.partial(gather_kernel, toks), out_shape=(jax.Sha...  113 us
    pallas_call x1, Pallas kernels, combine(): pl.pallas_call(combine_kernel, out_shape=(jax.ShapeDtypeStruct((SIDE, SID...  81.8 us
    pallas_call x1, Pallas kernels, spread(): pl.pallas_call(spread_kernel, out_shape=jax.ShapeDtypeStruct((4, 2, share...  36.9 us

profile of v2, /device:TPU:1, one launch (start us, length us, event | category | flops | bytes accessed | tf_op | source)
XLA Modules:
  0.0 448.1 jit_solution(10130519162896885060)
XLA Ops:
  0.0 0.7 compare_reduce_fusion
  0.7 2.3 bitcast_select_fusion.x_hbm
  3.0 112.8 %gather.1 = (f32[512,2048]{1,0:T(8,128)}, f32[128,2048]{1,0:T(8,128)}) custom-call(bf16[256,2048]{1,0:T(8,128)(2,1)} %bitcast_select_fusion.x_hbm, s32[2,128]{1,0:T(2,128)} %bitcast.14, bf16[2048,512]{1,0:T(8,128)(2,1)} %bitcast.12), custom_call_target="tpu_custom_call" | custom-call | tf_op jit(solution)/shard_map/gather/pallas_call | solution.py:222
  115.9 81.8 %combine.1 = (f32[4,4,2,2,32,2048]{5,4,3,2,1,0:T(8,128)}, f32[64,2048]{1,0:T(8,128)}) custom-call(f32[2,4,16,2048]{3,2,1,0:T(8,128)} %bitcast.13, f32[4,2,64,2048]{3,2,1,0:T(8,128)} %bitcast.11), custom_call_target="tpu_custom_call" | custom-call | tf_op jit(solution)/shard_map/combine/pallas_call | solution.py:358
  197.7 208.1 %solve.1.a_ref = f32[64,2048]{1,0:T(8,128)} custom-call(f32[2048,2048]{1,0:T(8,128)} %bitcast.9, f32[64,2048]{1,0:T(8,128)} %get-tuple-element.12.b_in), custom_call_target="tpu_custom_call" | custom-call | tf_op jit(solution)/shard_map/solve/pallas_call | solution.py:587
  405.8 36.9 %spread.1 = f32[4,2,64,2048]{3,2,1,0:T(8,128)} custom-call(f32[64,2048]{1,0:T(8,128)} %solve.1.a_ref), custom_call_target="tpu_custom_call" | custom-call | tf_op jit(solution)/shard_map/spread/pallas_call | solution.py:427
  442.7 5.3 %copy.4 = f32[512,2048]{0,1:T(8,128)} copy(f32[512,2048]{1,0:T(8,128)} %bitcast.10) | data formatting | bytes 8388608 | tf_op jit(solution)/shard_map/reshape | solution.py:436
